TPU v7x, 512 devices: a whole 4x4x16 slice. The times are simulated.
512 devices in a mesh: row: 32 (over y, z_hi, core), col: 16 (over x, z_lo).
Axes of the slice: x: 4, y: 4, z: 16 (z_hi: 4, z_lo: 4; z = z_hi * 4 + z_lo), core: 2. Of those that a mesh axis runs over, the one named last changes fastest.
Arguments:
- inputs: bfloat16 [512, 8192], P('row', 'col'), may hold values from -6 to 6
- out_grad: bfloat16 [512, 8192], P('row', 'col'), may hold values from -1.5 to 1.5
- gate_weight: bfloat16 [8192, 16384], P('col', 'row'), may hold values from -0.0625 to 0.0625
- up_weight: bfloat16 [8192, 16384], P('col', 'row'), may hold values from -0.0625 to 0.0625
- down_weight: bfloat16 [16384, 8192], P('row', 'col'), may hold values from -0.046875 to 0.046875
Outputs:
- input_grad: bfloat16 [512, 8192], P('row', 'col')
- gate_weight_grad: bfloat16 [8192, 16384], P('col', 'row')
- up_weight_grad: bfloat16 [8192, 16384], P('col', 'row')
- down_weight_grad: bfloat16 [16384, 8192], P('row', 'col')
All inputs are finite; a program needn't handle non-finite values.
Results may differ from a plain program's by a relative error of at most 0.0095.
Values may be sent and summed in bfloat16 or wider, within the bound.
A program may use at most 64 MiB of HBM per device.

v0:
```python
import jax
import jax.numpy as jnp
from jax import lax
from jax.sharding import PartitionSpec as P


def swiglu_back(gate, up_proj, hid_grad):
    sigma = jax.nn.sigmoid(gate)
    silu_gate = gate * sigma
    hidden = (silu_gate * up_proj).astype(jnp.bfloat16)
    up_grad = (hid_grad * silu_gate).astype(jnp.bfloat16)
    gate_grad = (hid_grad * up_proj * sigma * (1.0 + gate * (1.0 - sigma))).astype(jnp.bfloat16)
    return (hidden, gate_grad, up_grad)


def body(inputs, out_grad, gate_weight, up_weight, down_weight):
    gathered_in, gathered_grad = (
        lax.all_gather(inputs, "row", axis=0, tiled=True),
        lax.all_gather(out_grad, "row", axis=0, tiled=True),
    )
    hidden_width = gate_weight.shape[1]
    contract_last = (((1,), (1,)), ((), ()))
    contract_rows = (((0,), (0,)), ((), ()))
    gate_part = jnp.dot(gathered_in, gate_weight, preferred_element_type=jnp.float32)
    up_part = jnp.dot(gathered_in, up_weight, preferred_element_type=jnp.float32)
    hid_part = lax.dot_general(
        gathered_grad, down_weight, contract_last, preferred_element_type=jnp.float32
    )
    totals = lax.psum_scatter(
        jnp.concatenate([gate_part, up_part, hid_part], axis=1),
        "col",
        scatter_dimension=0,
        tiled=True,
    )
    hidden, gate_grad, up_grad = swiglu_back(
        totals[:, :hidden_width],
        totals[:, hidden_width : 2 * hidden_width],
        totals[:, 2 * hidden_width :],
    )
    hidden_all, gate_grad_all, up_grad_all = (
        lax.all_gather(hidden, "col", axis=0, tiled=True),
        lax.all_gather(gate_grad, "col", axis=0, tiled=True),
        lax.all_gather(up_grad, "col", axis=0, tiled=True),
    )
    down_weight_grad = lax.dot_general(
        hidden_all, gathered_grad, contract_rows, preferred_element_type=jnp.float32
    ).astype(jnp.bfloat16)
    gate_weight_grad = lax.dot_general(
        gathered_in, gate_grad_all, contract_rows, preferred_element_type=jnp.float32
    ).astype(jnp.bfloat16)
    up_weight_grad = lax.dot_general(
        gathered_in, up_grad_all, contract_rows, preferred_element_type=jnp.float32
    ).astype(jnp.bfloat16)
    first_term = lax.dot_general(
        gate_grad_all, gate_weight, contract_last, preferred_element_type=jnp.float32
    )
    second_term = lax.dot_general(
        up_grad_all, up_weight, contract_last, preferred_element_type=jnp.float32
    )
    input_grad = lax.psum_scatter(
        first_term + second_term, "row", scatter_dimension=0, tiled=True
    ).astype(jnp.bfloat16)
    return (input_grad, gate_weight_grad, up_weight_grad, down_weight_grad)


def solution(mesh):
    placed = (P("row", "col"), P("row", "col"), P("col", "row"), P("col", "row"), P("row", "col"))
    return jax.shard_map(
        body,
        mesh=mesh,
        in_specs=placed,
        out_specs=(P("row", "col"), P("col", "row"), P("col", "row"), P("row", "col")),
        check_vma=False,
    )
```

profile of v0, /device:TPU:1, one launch (start us, length us, event | category | flops | bytes accessed | tf_op | source)
XLA Modules:
  0.0 429.7 jit_solution(17388630047997059129)
XLA Ops:
  7.2 0.0 reduce-scatter.7.cloned.1.call-start
  7.2 63.1 %all_gather.15 = bf16[512,512]{1,0:T(8,128)(2,1)S(1)} all-gather(bf16[16,512]{1,0:T(8,128)(2,1)} %param.5), channel_id=1, replica_groups=mesh['row'=32,'col'=16] {'row'}, dimensions={0}, use_global_device_ids=true | all-gather | bytes 540672 | tf_op jit(solution)/shard_map/all_gather | solution.py:18
  70.3 48.6 %all_gather.16 = bf16[512,512]{1,0:T(8,128)(2,1)S(1)} all-gather(bf16[16,512]{1,0:T(8,128)(2,1)} %param.6), channel_id=1, replica_groups=mesh['row'=32,'col'=16] {'row'}, dimensions={0}, use_global_device_ids=true | all-gather | bytes 540672 | tf_op jit(solution)/shard_map/all_gather | solution.py:19
  118.9 1.5 fusion.4
  120.5 0.5 fusion.3
  121.0 0.5 fusion.5
  121.4 2.0 pad_maximum_fusion
  123.4 3.5 copy.21
  127.0 0.0 reduce-scatter.7.cloned.1.call-update
  127.0 0.0 reduce-scatter.5.cloned.1.call-start
  127.0 85.2 %reduce-scatter.7.cloned.1.call-done = f32[32,1536]{1,0:T(8,128)} async-done(((f32[512,1536]{1,0:T(8,128)}), f32[32,1536]{1,0:T(8,128)}) %reduce-scatter.7.cloned.1.call-update) | async-done | bytes 196624 | tf_op jit(solution)/shard_map/reduce_scatter | solution.py:29
  212.2 1.0 multiply_convert_fusion
  213.1 37.5 %all_gather.18 = bf16[512,512]{1,0:T(8,128)(2,1)S(1)} all-gather(bf16[32,512]{1,0:T(8,128)(2,1)S(1)} %get-tuple-element.17), channel_id=1, replica_groups=mesh['row'=32,'col'=16] {'col'}, dimensions={0}, use_global_device_ids=true | all-gather | bytes 557056 | tf_op jit(solution)/shard_map/all_gather | solution.py:43
  250.7 34.5 %all_gather.17 = bf16[512,512]{1,0:T(8,128)(2,1)S(1)} all-gather(bf16[32,512]{1,0:T(8,128)(2,1)S(1)} %get-tuple-element.18), channel_id=1, replica_groups=mesh['row'=32,'col'=16] {'col'}, dimensions={0}, use_global_device_ids=true | all-gather | bytes 557056 | tf_op jit(solution)/shard_map/all_gather | solution.py:42
  285.1 0.5 fusion.6
  285.6 1.4 convolution_add_fusion
  287.1 0.5 fusion.1
  287.6 1.0 copy.20
  288.6 0.5 fusion
  289.0 1.0 copy.19
  290.0 37.8 %all_gather.19 = bf16[512,512]{1,0:T(8,128)(2,1)S(1)} all-gather(bf16[32,512]{1,0:T(8,128)(2,1)S(1)} %get-tuple-element.16), channel_id=1, replica_groups=mesh['row'=32,'col'=16] {'col'}, dimensions={0}, use_global_device_ids=true | all-gather | bytes 557056 | tf_op jit(solution)/shard_map/all_gather | solution.py:41
  327.9 1.3 convolution_convert_fusion
  329.1 92.4 %reduce-scatter.5.cloned.1.call-done = f32[16,512]{1,0:T(8,128)} async-done(((f32[512,512]{1,0:T(8,128)}), f32[16,512]{1,0:T(8,128)}) %reduce-scatter.5.cloned.1.call-update) | async-done | bytes 32784 | tf_op jit(solution)/shard_map/reduce_scatter | solution.py:60
  421.5 1.4 convert_element_type.29
  (7 shorter events, 0.0 us)
Async XLA Ops:
  7.2 113.3 %copy-start = (bf16[512,512]{1,0:T(8,128)(2,1)S(1)}, bf16[512,512]{1,0:T(8,128)(2,1)}, u32[]{:S(2)}) copy-start(bf16[512,512]{1,0:T(8,128)(2,1)} %param.7) | copy-start | bytes 1572868
  7.2 113.8 %copy-start.2 = (bf16[512,512]{1,0:T(8,128)(2,1)S(1)}, bf16[512,512]{1,0:T(8,128)(2,1)}, u32[]{:S(2)}) copy-start(bf16[512,512]{1,0:T(8,128)(2,1)} %param.9) | copy-start | bytes 1572868
  7.2 205.0 %reduce-scatter.7.cloned.1.call-start = ((), (), s32[]{:S(2)}) async-start(), calls=%async_computation.3 | async-start | bytes 3342336 | tf_op jit(solution)/shard_map/reduce_scatter | solution.py:29
  126.9 158.7 %copy-start.1 = (bf16[512,512]{1,0:T(8,128)(2,1)S(1)}, bf16[512,512]{1,0:T(8,128)(2,1)}, u32[]{:S(2)}) copy-start(bf16[512,512]{1,0:T(8,128)(2,1)} %param.8) | copy-start | bytes 1572868
  127.0 294.6 %reduce-scatter.5.cloned.1.call-start = ((), (), s32[]{:S(2)}) async-start(), calls=%async_computation.2 | async-start | bytes 1081344 | tf_op jit(solution)/shard_map/reduce_scatter | solution.py:60
Sparse Core Ops, SparseCore 0:
  127.1 85.0 reduce-scatter.6
  287.2 134.2 reduce-scatter.4
where the time goes:
time: 431 us; the launch traced here: 430 us
  blocking collectives  222 us (52%)
  waiting for transfers between devices  178 us (41%)
  between operations  14.1 us (3%)
  matrix products  6.57 us (2%)
  local copies, waits for them, and re-layouts  5.55 us (1%)
    reduce_scatter x1, waiting for transfers between devices, body(): lax.psum_scatter(first_term + second_term, 'row', scatter_dimension=0, ti...  92.4 us
    reduce_scatter x1, waiting for transfers between devices, body(): lax.psum_scatter(jnp.concatenate([gate_part, up_part, hid_part], axis=1),...  85.2 us
    all_gather x1, blocking collectives, body(): lax.all_gather(inputs, 'row', axis=0, tiled=True)  63.1 us
    all_gather x1, blocking collectives, body(): lax.all_gather(out_grad, 'row', axis=0, tiled=True)  48.6 us
    all_gather x1, blocking collectives, body(): lax.all_gather(hidden, 'col', axis=0, tiled=True)  37.8 us
    all_gather x1, blocking collectives, body(): lax.all_gather(up_grad, 'col', axis=0, tiled=True)  37.5 us
    all_gather x1, blocking collectives, body(): lax.all_gather(gate_grad, 'col', axis=0, tiled=True)  34.5 us
  transfers between devices with their start and end apart: 2, of which 2 were waited for; matrix products, arithmetic and copies ran while one was open for 1% of the time, Pallas kernels for 0%

commit v1 on v0

v1 whole, which is shorter than its diff:
```python
import jax
import jax.numpy as jnp
from jax import lax
from jax.experimental import pallas as pl
from jax.experimental.pallas import tpu as pltpu
from jax.sharding import PartitionSpec as P

F32 = jnp.float32
BF16 = jnp.bfloat16
LAST = (((1,), (1,)), ((), ()))
ROWS = (((0,), (0,)), ((), ()))

Y_OFF = (0, 1, 3, 2)


class Sems:
    def __init__(self):
        self.names = {}

    def __getitem__(self, name):
        return self.names.setdefault(name, len(self.names))


N_SEMS = 160


def swiglu_back(gate, up_proj, hid_grad):
    sigma = jax.nn.sigmoid(gate)
    silu_gate = gate * sigma
    hidden = (silu_gate * up_proj).astype(BF16)
    up_grad = (hid_grad * silu_gate).astype(BF16)
    gate_grad = (hid_grad * up_proj * sigma * (1.0 + gate * (1.0 - sigma))).astype(BF16)
    return hidden, gate_grad, up_grad


def kernel(
    in_ref, og_ref, wg_ref, wu_ref, wd_ref,
    dx_ref, dwg_ref, dwu_ref, dwd_ref,
    XG, WG, WU, WD, PP, RX, Z, ZR, HGU, DXF, DXS, SR, YF, YS, YR, ZS, ZHR, OUT, DW,
    send_sem, recv_sem, local_sem,
):
    row = lax.axis_index("row")
    col = lax.axis_index("col")
    y, zh, core = row // 8, (row // 2) % 4, row % 2
    x, zl = col // 4, col % 4

    def at_row(yy, hh, cc):
        return (yy * 8 + hh * 2 + cc, col)

    def ypeer(d):
        return at_row((y + d) % 4, zh, core)

    def hpeer(d):
        return at_row(y, (zh + d) % 4, core)

    def xpeer(d):
        return (row, ((x + d) % 4) * 4 + zl)

    def lpeer(d):
        return (row, x * 4 + (zl + d) % 4)

    sib = at_row(y, zh, 1 - core)

    sems = Sems()
    pending = []

    def desc(name, src, dst, dev):
        i = sems[name]
        return pltpu.make_async_remote_copy(
            src_ref=src, dst_ref=dst, send_sem=send_sem.at[i], recv_sem=recv_sem.at[i],
            device_id=dev, device_id_type=pl.DeviceIdType.MESH,
        )

    started = {}

    def send(name, src, dst, dev):
        d = desc(name, src, dst, dev)
        d.start()
        started[name] = d

    def recv(name):
        started[name].wait_recv()

    loads = []
    for i, (src, dst) in enumerate((
        (in_ref, XG.at[0, 0, 0, 0]), (og_ref, XG.at[1, 0, 0, 0]),
        (wg_ref, WG), (wu_ref, WU), (wd_ref, WD),
    )):
        c = pltpu.make_async_copy(src, dst, local_sem.at[i])
        c.start()
        loads.append(c)

    barrier = pltpu.get_barrier_semaphore()
    peers = [sib] + [ypeer(d) for d in (1, 2, 3)] + [hpeer(d) for d in (1, 2, 3)]
    peers += [xpeer(1), xpeer(3)] + [lpeer(d) for d in (1, 2, 3)]
    for p in peers:
        pl.semaphore_signal(barrier, inc=1, device_id=p, device_id_type=pl.DeviceIdType.MESH)
    pl.semaphore_wait(barrier, len(peers))
    loads[0].wait()
    loads[1].wait()

    def spread(js, tag):
        src = XG.at[:, 0, 0, js]
        send("yp" + tag, src, XG.at[:, 2, 0, js], ypeer(1))
        send("ym" + tag, src, XG.at[:, 1, 0, js], ypeer(3))
        send("sib0" + tag, src, XG.at[:, 0, 1, js], sib)

    own = XG.at[:, 0, 0, 0]
    send("hp", own, XG.at[:, 0, 0, 2], hpeer(1))
    send("hm", own, XG.at[:, 0, 0, 1], hpeer(3))
    spread(pl.ds(0, 1), "0")
    recv("hp")
    send("hpp", XG.at[0, 0, 0, 2], XG.at[0, 0, 0, 3], hpeer(1))
    recv("hm")
    send("hmm", XG.at[1, 0, 0, 1], XG.at[1, 0, 0, 3], hpeer(3))
    spread(pl.ds(1, 2), "12")
    recv("hpp")
    recv("hmm")
    spread(pl.ds(3, 1), "3")
    tags = ("0", "12", "3")

    def a_near():
        for t in tags:
            recv("ym" + t)
        send("ymm", XG.at[1, 1, 0], XG.at[1, 3, 0], ypeer(3))
        send("sib1", XG.at[:, 1, 0], XG.at[:, 1, 1], sib)
        for t in tags:
            recv("yp" + t)
        send("ypp", XG.at[0, 2, 0], XG.at[0, 3, 0], ypeer(1))
        send("sib2", XG.at[:, 2, 0], XG.at[:, 2, 1], sib)

    def a_far():
        recv("ymm")
        recv("ypp")
        send("sib3", XG.at[:, 3, 0], XG.at[:, 3, 1], sib)

    xp, xm = (x + 1) % 4, (x + 3) % 4
    xf = (x + 2) % 4

    def s1(k):
        if k == 0:
            for t in tags:
                recv("sib0" + t)
            for c in loads[2:]:
                c.wait()
        else:
            recv("sib%d" % k)
        xk = XG[0, k].reshape(128, 512)
        gk = XG[1, k].reshape(128, 512)
        parts = (
            jnp.dot(xk, WG[...], preferred_element_type=F32),
            jnp.dot(xk, WU[...], preferred_element_type=F32),
            lax.dot_general(gk, WD[...], LAST, preferred_element_type=F32),
        )
        for i, part in enumerate(parts):
            part = part.astype(BF16)
            for q in range(4):
                PP[k, :, :, q, :, 128 * i:128 * (i + 1)] = (
                    part[:, 128 * q:128 * (q + 1)].reshape(4, 2, 16, 128))
        send("far+%d" % k, PP.at[k, xf, 0], RX.at[k, 0], xpeer(1))
        send("far-%d" % k, PP.at[k, xf, 1], RX.at[k, 1], xpeer(3))
        send("dir+%d" % k, PP.at[k, xp, 1], RX.at[k, 4], xpeer(1))
        send("dir-%d" % k, PP.at[k, xm, 0], RX.at[k, 3], xpeer(3))

    def s2(k):
        recv("far+%d" % k)
        PP[k, xp, 0] = (PP[k, xp, 0].astype(F32) + RX[k, 0].astype(F32)).astype(BF16)
        send("acc+%d" % k, PP.at[k, xp, 0], RX.at[k, 2], xpeer(1))
        recv("far-%d" % k)
        PP[k, xm, 1] = (PP[k, xm, 1].astype(F32) + RX[k, 1].astype(F32)).astype(BF16)
        send("acc-%d" % k, PP.at[k, xm, 1], RX.at[k, 5], xpeer(3))

    def s3(k):
        for n in ("dir+", "dir-", "acc+", "acc-"):
            recv(n + str(k))
        for h in range(2):
            Z[k, h] = (PP[k, x, h].astype(F32) + RX[k, 2 + 2 * h].astype(F32)
                       + RX[k, 3 + 2 * h].astype(F32)).astype(BF16)
        for m in (1, 2, 3):
            send("z%d%d" % (m, k), Z.at[k, :, (zl + m) % 4], ZR.at[k, m - 1], lpeer(m))

    def s4(k):
        for m in (1, 2, 3):
            recv("z%d%d" % (m, k))
        total = (Z[k, :, zl].astype(F32) + ZR[k, 0].astype(F32)
                 + ZR[k, 1].astype(F32) + ZR[k, 2].astype(F32))
        hidden, gate_grad, up_grad = swiglu_back(
            total[:, :, :128], total[:, :, 128:256], total[:, :, 256:])
        HGU[k, x, :, zl, :, 0:128] = hidden
        HGU[k, x, :, zl, :, 128:256] = gate_grad
        HGU[k, x, :, zl, :, 256:384] = up_grad
        for m in (1, 2, 3):
            mine = HGU.at[k, x, :, zl]
            send("g%d%d" % (m, k), mine, mine, lpeer(m))

    def s5(k):
        for m in (1, 2, 3):
            recv("g%d%d" % (m, k))
        mine = HGU.at[k, x]
        send("ag+%d" % k, mine, mine, xpeer(1))
        send("ag-%d" % k, mine, mine, xpeer(3))

    def s6(k):
        recv("ag+%d" % k)
        fwd = HGU.at[k, xm, 0]
        send("af+%d" % k, fwd, fwd, xpeer(1))
        recv("ag-%d" % k)
        fwd = HGU.at[k, xp, 1]
        send("af-%d" % k, fwd, fwd, xpeer(3))

    def cols(k, i):
        lead = (128,) if not isinstance(k, slice) else (512,)
        return jnp.concatenate(
            [HGU[k, :, :, q, :, 128 * i:128 * (i + 1)].reshape(lead + (128,)) for q in range(4)], axis=-1)

    def s7(k):
        recv("af+%d" % k)
        recv("af-%d" % k)
        dx = (lax.dot_general(cols(k, 1), WG[...], LAST, preferred_element_type=F32)
              + lax.dot_general(cols(k, 2), WU[...], LAST, preferred_element_type=F32))
        DXF[k] = dx[:64].reshape(4, 16, 512)
        DXS[k] = dx[64:].astype(BF16).reshape(4, 16, 512)
        send("f1%d" % k, DXS.at[k], SR.at[k], sib)

    def s8(k):
        recv("f1%d" % k)
        total = DXF[k] + SR[k].astype(F32)
        if k == 0:
            YF[...] = total
        else:
            YS[k - 1] = total.astype(BF16)
            send("f2%d" % k, YS.at[k - 1], YR.at[k - 1], ypeer(Y_OFF[k]))

    def s9():
        for k in (1, 2, 3):
            recv("f2%d" % k)
        total = YF[...] + YR[0].astype(F32) + YR[1].astype(F32) + YR[2].astype(F32)
        YF[...] = total
        for j, d in ((1, 1), (2, 3), (3, 2)):
            ZS[j - 1] = total[j].astype(BF16)
            send("f3%d" % j, ZS.at[j - 1], ZHR.at[j - 1], hpeer(d))

    def wgrads():
        al = slice(None)
        stores = []
        X = XG[0].reshape(512, 512)
        G = XG[1].reshape(512, 512)
        for i, (a, b, out) in enumerate((
            (cols(al, 0), G, dwd_ref), (X, cols(al, 1), dwg_ref), (X, cols(al, 2), dwu_ref),
        )):
            DW[i] = lax.dot_general(a, b, ROWS, preferred_element_type=F32).astype(BF16)
            c = pltpu.make_async_copy(DW.at[i], out, local_sem.at[5 + i])
            c.start()
            stores.append(c)
        return stores

    s1(0)
    a_near()
    s1(1)
    s2(0)
    s1(2)
    s2(1)
    a_far()
    s3(0)
    s1(3)
    s2(2)
    s3(1)
    s4(0)
    s2(3)
    s3(2)
    s4(1)
    s5(0)
    s3(3)
    s4(2)
    s5(1)
    s6(0)
    s4(3)
    s5(2)
    s6(1)
    s7(0)
    s5(3)
    s6(2)
    s7(1)
    s8(0)
    s6(3)
    s7(2)
    s8(1)
    s7(3)
    s8(2)
    s8(3)
    stores = wgrads()
    s9()
    for j in (1, 2, 3):
        recv("f3%d" % j)
    OUT[...] = (YF[0] + ZHR[0].astype(F32) + ZHR[1].astype(F32) + ZHR[2].astype(F32)).astype(BF16)
    c = pltpu.make_async_copy(OUT, dx_ref, local_sem.at[8])
    c.start()
    stores.append(c)
    for d in started.values():
        d.wait_send()
    for c in stores:
        c.wait()


def body(inputs, out_grad, gate_weight, up_weight, down_weight):
    any_spec = pl.BlockSpec(memory_space=pl.ANY)
    S = jax.ShapeDtypeStruct
    return tuple(pl.pallas_call(
        kernel,
        out_shape=(S((16, 512), BF16), S((512, 512), BF16), S((512, 512), BF16), S((512, 512), BF16)),
        in_specs=[any_spec] * 5,
        out_specs=(any_spec,) * 4,
        scratch_shapes=[
            pltpu.VMEM((2, 4, 2, 4, 16, 512), BF16),
            pltpu.VMEM((512, 512), BF16),
            pltpu.VMEM((512, 512), BF16),
            pltpu.VMEM((512, 512), BF16),
            pltpu.VMEM((4, 4, 2, 4, 16, 384), BF16),
            pltpu.VMEM((4, 6, 4, 16, 384), BF16),
            pltpu.VMEM((4, 2, 4, 16, 384), BF16),
            pltpu.VMEM((4, 3, 2, 16, 384), BF16),
            pltpu.VMEM((4, 4, 2, 4, 16, 384), BF16),
            pltpu.VMEM((4, 4, 16, 512), F32),
            pltpu.VMEM((4, 4, 16, 512), BF16),
            pltpu.VMEM((4, 4, 16, 512), BF16),
            pltpu.VMEM((4, 16, 512), F32),
            pltpu.VMEM((3, 4, 16, 512), BF16),
            pltpu.VMEM((3, 4, 16, 512), BF16),
            pltpu.VMEM((3, 16, 512), BF16),
            pltpu.VMEM((3, 16, 512), BF16),
            pltpu.VMEM((16, 512), BF16),
            pltpu.VMEM((3, 512, 512), BF16),
            pltpu.SemaphoreType.DMA((N_SEMS,)),
            pltpu.SemaphoreType.DMA((N_SEMS,)),
            pltpu.SemaphoreType.DMA((9,)),
        ],
        compiler_params=pltpu.CompilerParams(
            collective_id=0, has_side_effects=True, vmem_limit_bytes=48 * 1024 * 1024),
    )(inputs, out_grad, gate_weight, up_weight, down_weight))


def solution(mesh):
    placed = (P("row", "col"), P("row", "col"), P("col", "row"), P("col", "row"), P("row", "col"))
    return jax.shard_map(
        body,
        mesh=mesh,
        in_specs=placed,
        out_specs=(P("row", "col"), P("col", "row"), P("col", "row"), P("row", "col")),
        check_vma=False,
    )
```

time: 431 us -> 92.1 us (0.21)
  blocking collectives: 222 us -> 0 us
  waiting for transfers between devices: 178 us -> 0 us
  Pallas kernels: 0 us -> 83.6 us
  between operations: 14.1 us -> 0.65 us
  matrix products: 6.57 us -> 0 us
    all_gather x5 -> x0, blocking collectives: 222 us -> none  [the longest x1 63.1 us: body(): lax.all_gather(inputs, 'row', axis=0, tiled=True)]
    reduce_scatter x2 -> x0, waiting for transfers between devices: 178 us -> none  [the longest x1 92.4 us: body(): lax.psum_scatter(first_term + second_term, 'row', scatter_dimension=0, ti...]
    pallas_call x0 -> x1, Pallas kernels: none -> 83.6 us  [body(): pl.pallas_call(kernel, out_shape=(S((16, 512), BF16), S((512, 512), BF16)...]
    dot_general x8 -> x0, matrix products: 6.57 us -> none  [the longest x1 1.52 us: body(): jnp.dot(gathered_in, up_weight, preferred_element_type=jnp.float32)]
  transfers between devices with their start and end apart: 2 -> 0, of which waited for: 2 -> 0; matrix products, arithmetic and copies ran while one was open for 1% -> 0% of each run, Pallas kernels for 0% -> 0%
where the time goes in v1:
time: 92.1 us; the launch traced here: 91.8 us
  Pallas kernels  83.6 us (91%)
  local copies, waits for them, and re-layouts  7.54 us (8%)
    pallas_call x1, Pallas kernels, body(): pl.pallas_call(kernel, out_shape=(S((16, 512), BF16), S((512, 512), BF16)...  83.6 us
    unnamed x14, local copies, waits for them, and re-layouts  7.54 us

profile of v1, /device:TPU:1, one launch (start us, length us, event | category | flops | bytes accessed | tf_op | source)
XLA Modules:
  0.0 91.8 jit_solution(8759892176720576869)
XLA Ops:
  0.6 0.0 copy-start
  0.6 1.0 %copy-done = bf16[512,512]{1,0:T(8,128)(2,1)S(1)} copy-done((bf16[512,512]{1,0:T(8,128)(2,1)S(1)}, bf16[512,512]{1,0:T(8,128)(2,1)}, u32[]{:S(2)}) %copy-start) | copy-done | bytes 524312
  1.7 0.0 copy-start.1
  1.7 1.0 %copy-done.1 = bf16[512,512]{1,0:T(8,128)(2,1)S(1)} copy-done((bf16[512,512]{1,0:T(8,128)(2,1)S(1)}, bf16[512,512]{1,0:T(8,128)(2,1)}, u32[]{:S(2)}) %copy-start.1) | copy-done | bytes 524312
  2.7 0.0 copy-start.2
  2.7 1.0 %copy-done.2 = bf16[512,512]{1,0:T(8,128)(2,1)S(1)} copy-done((bf16[512,512]{1,0:T(8,128)(2,1)S(1)}, bf16[512,512]{1,0:T(8,128)(2,1)}, u32[]{:S(2)}) %copy-start.2) | copy-done | bytes 524312
  3.8 0.0 copy-start.3
  3.8 0.7 copy-done.3
  4.5 0.0 copy-start.4
  4.5 0.7 copy-done.4
  5.2 83.6 %shard_map.84 = (bf16[16,512]{1,0:T(8,128)(2,1)S(1)}, bf16[512,512]{1,0:T(8,128)(2,1)S(1)}, bf16[512,512]{1,0:T(8,128)(2,1)S(1)}, bf16[512,512]{1,0:T(8,128)(2,1)S(1)}) custom-call(bf16[16,512]{1,0:T(8,128)(2,1)S(1)} %copy-done.3, bf16[16,512]{1,0:T(8,128)(2,1)S(1)} %copy-done.4, bf16[512,512]{1,0:T(8,128)(2,1)S(1)} %copy-done, ...), custom_call_target="tpu_custom_call" | custom-call | tf_op jit(solution)/shard_map/pallas_call | solution.py:308
  88.8 0.6 copy.13
  89.4 0.8 copy.14
  90.2 0.8 copy.15
  91.0 0.8 copy.16
Async XLA Ops:
  0.6 1.0 %copy-start = (bf16[512,512]{1,0:T(8,128)(2,1)S(1)}, bf16[512,512]{1,0:T(8,128)(2,1)}, u32[]{:S(2)}) copy-start(bf16[512,512]{1,0:T(8,128)(2,1)} %wg_ref.1) | copy-start | bytes 1572868
  1.7 1.0 %copy-start.1 = (bf16[512,512]{1,0:T(8,128)(2,1)S(1)}, bf16[512,512]{1,0:T(8,128)(2,1)}, u32[]{:S(2)}) copy-start(bf16[512,512]{1,0:T(8,128)(2,1)} %wu_ref.1) | copy-start | bytes 1572868
  2.7 1.0 %copy-start.2 = (bf16[512,512]{1,0:T(8,128)(2,1)S(1)}, bf16[512,512]{1,0:T(8,128)(2,1)}, u32[]{:S(2)}) copy-start(bf16[512,512]{1,0:T(8,128)(2,1)} %wd_ref.1) | copy-start | bytes 1572868
  3.8 0.7 copy-start.3
  4.5 0.7 copy-start.4

commit v2 on v1

--- a/solution.py
+++ b/solution.py
@@ -7,10 +7,9 @@
 
 F32 = jnp.float32
 BF16 = jnp.bfloat16
-LAST = (((1,), (1,)), ((), ()))
 ROWS = (((0,), (0,)), ((), ()))
 
-Y_OFF = (0, 1, 3, 2)
+OFF = (0, 1, 3, 2)
 
 
 class Sems:
@@ -21,7 +20,7 @@
         return self.names.setdefault(name, len(self.names))
 
 
-N_SEMS = 160
+N_SEMS = 200
 
 
 def swiglu_back(gate, up_proj, hid_grad):
@@ -36,7 +35,7 @@
 def kernel(
     in_ref, og_ref, wg_ref, wu_ref, wd_ref,
     dx_ref, dwg_ref, dwu_ref, dwd_ref,
-    XG, WG, WU, WD, PP, RX, Z, ZR, HGU, DXF, DXS, SR, YF, YS, YR, ZS, ZHR, OUT, DW,
+    XG, WG, WU, WD, WGT, WUT, WDT, PP, RX, Z, ZR, HGU, DXF, DXS, SR, YF, ZS, ZHR, OUT, DW,
     send_sem, recv_sem, local_sem,
 ):
     row = lax.axis_index("row")
@@ -47,8 +46,8 @@
     def at_row(yy, hh, cc):
         return (yy * 8 + hh * 2 + cc, col)
 
-    def ypeer(d):
-        return at_row((y + d) % 4, zh, core)
+    def ypeer(d, c=0):
+        return at_row((y + d) % 4, zh, (core + c) % 2)
 
     def hpeer(d):
         return at_row(y, (zh + d) % 4, core)
@@ -62,8 +61,6 @@
     sib = at_row(y, zh, 1 - core)
 
     sems = Sems()
-    pending = []
-
     def desc(name, src, dst, dev):
         i = sems[name]
         return pltpu.make_async_remote_copy(
@@ -91,7 +88,7 @@
         loads.append(c)
 
     barrier = pltpu.get_barrier_semaphore()
-    peers = [sib] + [ypeer(d) for d in (1, 2, 3)] + [hpeer(d) for d in (1, 2, 3)]
+    peers = [sib] + [ypeer(d, c) for d in (1, 2, 3) for c in (0, 1)] + [hpeer(d) for d in (1, 2, 3)]
     peers += [xpeer(1), xpeer(3)] + [lpeer(d) for d in (1, 2, 3)]
     for p in peers:
         pl.semaphore_signal(barrier, inc=1, device_id=p, device_id_type=pl.DeviceIdType.MESH)
@@ -99,58 +96,46 @@
     loads[0].wait()
     loads[1].wait()
 
-    def spread(js, tag):
-        src = XG.at[:, 0, 0, js]
-        send("yp" + tag, src, XG.at[:, 2, 0, js], ypeer(1))
-        send("ym" + tag, src, XG.at[:, 1, 0, js], ypeer(3))
-        send("sib0" + tag, src, XG.at[:, 0, 1, js], sib)
-
-    own = XG.at[:, 0, 0, 0]
-    send("hp", own, XG.at[:, 0, 0, 2], hpeer(1))
-    send("hm", own, XG.at[:, 0, 0, 1], hpeer(3))
-    spread(pl.ds(0, 1), "0")
-    recv("hp")
-    send("hpp", XG.at[0, 0, 0, 2], XG.at[0, 0, 0, 3], hpeer(1))
-    recv("hm")
-    send("hmm", XG.at[1, 0, 0, 1], XG.at[1, 0, 0, 3], hpeer(3))
-    spread(pl.ds(1, 2), "12")
-    recv("hpp")
-    recv("hmm")
-    spread(pl.ds(3, 1), "3")
-    tags = ("0", "12", "3")
-
-    def a_near():
-        for t in tags:
-            recv("ym" + t)
-        send("ymm", XG.at[1, 1, 0], XG.at[1, 3, 0], ypeer(3))
-        send("sib1", XG.at[:, 1, 0], XG.at[:, 1, 1], sib)
-        for t in tags:
-            recv("yp" + t)
-        send("ypp", XG.at[0, 2, 0], XG.at[0, 3, 0], ypeer(1))
-        send("sib2", XG.at[:, 2, 0], XG.at[:, 2, 1], sib)
-
-    def a_far():
-        recv("ymm")
-        recv("ypp")
-        send("sib3", XG.at[:, 3, 0], XG.at[:, 3, 1], sib)
+    NEG = (0, 2, 1, 3)
+
+    def spread(k):
+        src = XG.at[:, k, 0, 0]
+        for c in (0, 1):
+            for s in (1, 2, 3):
+                send("y%d%d%d" % (k, c, s), src, XG.at[:, k, c, NEG[s]], ypeer(OFF[s], c))
+        send("s%d" % k, src, XG.at[:, k, 1, 0], sib)
+
+    spread(0)
+    for s in (1, 2, 3):
+        send("h%d" % s, XG.at[:, 0, 0, 0], XG.at[:, NEG[s], 0, 0], hpeer(OFF[s]))
+
+    def a_z(k):
+        recv("h%d" % NEG[k])
+        spread(k)
+
+    def weights():
+        for c in loads[2:]:
+            c.wait()
+        WDT[...] = WD[...].T
+
+    def weights2():
+        WGT[...] = WG[...].T
+        WUT[...] = WU[...].T
 
     xp, xm = (x + 1) % 4, (x + 3) % 4
     xf = (x + 2) % 4
 
     def s1(k):
-        if k == 0:
-            for t in tags:
-                recv("sib0" + t)
-            for c in loads[2:]:
-                c.wait()
-        else:
-            recv("sib%d" % k)
+        for c in (0, 1):
+            for t in (1, 2, 3):
+                recv("y%d%d%d" % (k, c, t))
+        recv("s%d" % k)
         xk = XG[0, k].reshape(128, 512)
         gk = XG[1, k].reshape(128, 512)
         parts = (
             jnp.dot(xk, WG[...], preferred_element_type=F32),
             jnp.dot(xk, WU[...], preferred_element_type=F32),
-            lax.dot_general(gk, WD[...], LAST, preferred_element_type=F32),
+            jnp.dot(gk, WDT[...], preferred_element_type=F32),
         )
         for i, part in enumerate(parts):
             part = part.astype(BF16)
@@ -216,90 +201,69 @@
     def s7(k):
         recv("af+%d" % k)
         recv("af-%d" % k)
-        dx = (lax.dot_general(cols(k, 1), WG[...], LAST, preferred_element_type=F32)
-              + lax.dot_general(cols(k, 2), WU[...], LAST, preferred_element_type=F32))
-        DXF[k] = dx[:64].reshape(4, 16, 512)
-        DXS[k] = dx[64:].astype(BF16).reshape(4, 16, 512)
-        send("f1%d" % k, DXS.at[k], SR.at[k], sib)
+        dx = (jnp.dot(cols(k, 1), WGT[...], preferred_element_type=F32)
+              + jnp.dot(cols(k, 2), WUT[...], preferred_element_type=F32))
+        DXF[k] = dx[:16]
+        DXS[k] = dx.astype(BF16).reshape(2, 4, 16, 512)
+        for c in (0, 1):
+            for s in (1, 2, 3):
+                send("f%d%d%d" % (k, c, s), DXS.at[k, c, s], SR.at[k, c, NEG[s]], ypeer(OFF[s], c))
+        send("f%d" % k, DXS.at[k, 1, 0], SR.at[k, 1, 0], sib)
 
     def s8(k):
-        recv("f1%d" % k)
-        total = DXF[k] + SR[k].astype(F32)
+        recv("f%d" % k)
+        total = DXF[k] + SR[k, 1, 0].astype(F32)
+        for c in (0, 1):
+            for s in (1, 2, 3):
+                recv("f%d%d%d" % (k, c, s))
+                total += SR[k, c, NEG[s]].astype(F32)
         if k == 0:
             YF[...] = total
         else:
-            YS[k - 1] = total.astype(BF16)
-            send("f2%d" % k, YS.at[k - 1], YR.at[k - 1], ypeer(Y_OFF[k]))
+            ZS[k - 1] = total.astype(BF16)
+            send("t%d" % k, ZS.at[k - 1], ZHR.at[k - 1], hpeer(OFF[k]))
 
     def s9():
+        total = YF[...]
         for k in (1, 2, 3):
-            recv("f2%d" % k)
-        total = YF[...] + YR[0].astype(F32) + YR[1].astype(F32) + YR[2].astype(F32)
-        YF[...] = total
-        for j, d in ((1, 1), (2, 3), (3, 2)):
-            ZS[j - 1] = total[j].astype(BF16)
-            send("f3%d" % j, ZS.at[j - 1], ZHR.at[j - 1], hpeer(d))
-
-    def wgrads():
+            recv("t%d" % k)
+            total += ZHR[k - 1].astype(F32)
+        OUT[...] = total.astype(BF16)
+        c = pltpu.make_async_copy(OUT, dx_ref, local_sem.at[8])
+        c.start()
+        stores.append(c)
+
+    stores = []
+
+    def wgrad(i):
         al = slice(None)
-        stores = []
         X = XG[0].reshape(512, 512)
         G = XG[1].reshape(512, 512)
-        for i, (a, b, out) in enumerate((
-            (cols(al, 0), G, dwd_ref), (X, cols(al, 1), dwg_ref), (X, cols(al, 2), dwu_ref),
-        )):
-            DW[i] = lax.dot_general(a, b, ROWS, preferred_element_type=F32).astype(BF16)
-            c = pltpu.make_async_copy(DW.at[i], out, local_sem.at[5 + i])
-            c.start()
-            stores.append(c)
-        return stores
-
-    s1(0)
-    a_near()
-    s1(1)
-    s2(0)
-    s1(2)
-    s2(1)
-    a_far()
-    s3(0)
-    s1(3)
-    s2(2)
-    s3(1)
-    s4(0)
-    s2(3)
-    s3(2)
-    s4(1)
-    s5(0)
-    s3(3)
-    s4(2)
-    s5(1)
-    s6(0)
-    s4(3)
-    s5(2)
-    s6(1)
-    s7(0)
-    s5(3)
-    s6(2)
-    s7(1)
-    s8(0)
-    s6(3)
-    s7(2)
-    s8(1)
-    s7(3)
-    s8(2)
-    s8(3)
-    stores = wgrads()
-    s9()
-    for j in (1, 2, 3):
-        recv("f3%d" % j)
-    OUT[...] = (YF[0] + ZHR[0].astype(F32) + ZHR[1].astype(F32) + ZHR[2].astype(F32)).astype(BF16)
-    c = pltpu.make_async_copy(OUT, dx_ref, local_sem.at[8])
-    c.start()
-    stores.append(c)
+        a, b, out = ((cols(al, 0), G, dwd_ref), (X, cols(al, 1), dwg_ref), (X, cols(al, 2), dwu_ref))[i]
+        DW[i] = lax.dot_general(a, b, ROWS, preferred_element_type=F32).astype(BF16)
+        c = pltpu.make_async_copy(DW.at[i], out, local_sem.at[5 + i])
+        c.start()
+        stores.append(c)
+
+    stages = dict(
+        s1=s1, s2=s2, s3=s3, s4=s4, s5=s5, s6=s6, s7=s7, s8=s8, s9=lambda _: s9(),
+        az=a_z, w=lambda i: (weights, weights2)[i](), wg=wgrad,
+    )
+    for name, k in SCHED:
+        stages[name](k)
     for d in started.values():
         d.wait_send()
     for c in stores:
         c.wait()
+
+
+SCHED = (
+    ("w", 0), ("s1", 0), ("az", 1), ("az", 2), ("s2", 0), ("az", 3), ("w", 1),
+    ("s1", 1), ("s3", 0), ("s1", 2), ("s2", 1), ("s1", 3), ("s2", 2), ("s4", 0), ("s3", 1), ("s2", 3),
+    ("s3", 2), ("s5", 0), ("s4", 1), ("s3", 3), ("s4", 2), ("s6", 0), ("s5", 1), ("s4", 3), ("s5", 2),
+    ("s7", 0), ("s6", 1), ("s5", 3), ("s6", 2), ("s7", 1), ("s6", 3), ("s8", 0), ("s7", 2), ("s8", 1),
+    ("s7", 3), ("wg", 0), ("s8", 2), ("s8", 3), ("wg", 1), ("wg", 2), ("s9", 0),
+)
 
 
 def body(inputs, out_grad, gate_weight, up_weight, down_weight):
@@ -308,10 +272,13 @@
     return tuple(pl.pallas_call(
         kernel,
         out_shape=(S((16, 512), BF16), S((512, 512), BF16), S((512, 512), BF16), S((512, 512), BF16)),
-        in_specs=[any_spec] * 5,
+        in_specs=[pl.BlockSpec(memory_space=pltpu.HBM)] * 5,
         out_specs=(any_spec,) * 4,
         scratch_shapes=[
             pltpu.VMEM((2, 4, 2, 4, 16, 512), BF16),
+            pltpu.VMEM((512, 512), BF16),
+            pltpu.VMEM((512, 512), BF16),
+            pltpu.VMEM((512, 512), BF16),
             pltpu.VMEM((512, 512), BF16),
             pltpu.VMEM((512, 512), BF16),
             pltpu.VMEM((512, 512), BF16),
@@ -320,12 +287,10 @@
             pltpu.VMEM((4, 2, 4, 16, 384), BF16),
             pltpu.VMEM((4, 3, 2, 16, 384), BF16),
             pltpu.VMEM((4, 4, 2, 4, 16, 384), BF16),
-            pltpu.VMEM((4, 4, 16, 512), F32),
-            pltpu.VMEM((4, 4, 16, 512), BF16),
-            pltpu.VMEM((4, 4, 16, 512), BF16),
             pltpu.VMEM((4, 16, 512), F32),
-            pltpu.VMEM((3, 4, 16, 512), BF16),
-            pltpu.VMEM((3, 4, 16, 512), BF16),
+            pltpu.VMEM((4, 2, 4, 16, 512), BF16),
+            pltpu.VMEM((4, 2, 4, 16, 512), BF16),
+            pltpu.VMEM((16, 512), F32),
             pltpu.VMEM((3, 16, 512), BF16),
             pltpu.VMEM((3, 16, 512), BF16),
             pltpu.VMEM((16, 512), BF16),
@@ -335,7 +300,7 @@
             pltpu.SemaphoreType.DMA((9,)),
         ],
         compiler_params=pltpu.CompilerParams(
-            collective_id=0, has_side_effects=True, vmem_limit_bytes=48 * 1024 * 1024),
+            collective_id=0, has_side_effects=True, vmem_limit_bytes=60 * 1024 * 1024),
     )(inputs, out_grad, gate_weight, up_weight, down_weight))
 
 

time: 92.1 us -> 81.6 us (0.89)
  Pallas kernels: 83.6 us -> 75.4 us
  local copies, waits for them, and re-layouts: 7.54 us -> 5.28 us
    pallas_call x1, Pallas kernels: 83.6 us -> 75.4 us  [body(): pl.pallas_call(kernel, out_shape=(S((16, 512), BF16), S((512, 512), BF16)...]
    unnamed x14 -> x8, local copies, waits for them, and re-layouts: 7.54 us -> 5.28 us
where the time goes in v2:
time: 81.6 us; the launch traced here: 81.3 us
  Pallas kernels  75.4 us (92%)
  local copies, waits for them, and re-layouts  5.28 us (6%)
    pallas_call x1, Pallas kernels, body(): pl.pallas_call(kernel, out_shape=(S((16, 512), BF16), S((512, 512), BF16)...  75.4 us
    unnamed x8, local copies, waits for them, and re-layouts  5.28 us

profile of v2, /device:TPU:1, one launch (start us, length us, event | category | flops | bytes accessed | tf_op | source)
XLA Modules:
  0.0 81.3 jit_solution(6122137626096016520)
XLA Ops:
  0.6 75.4 %shard_map.84 = (bf16[16,512]{1,0:T(8,128)(2,1)}, bf16[512,512]{1,0:T(8,128)(2,1)}, bf16[512,512]{1,0:T(8,128)(2,1)}, bf16[512,512]{1,0:T(8,128)(2,1)}) custom-call(bf16[16,512]{1,0:T(8,128)(2,1)} %in_ref.1, bf16[16,512]{1,0:T(8,128)(2,1)} %og_ref.1, bf16[512,512]{1,0:T(8,128)(2,1)} %wg_ref.1, bf16[512,512]{1,0:T(8,128)(2,1)} %wu_ref.1, bf16[512,512]{1,0:T(8,128)(2,1)} %wd_ref.1), custom_call_target="tpu_custom_call" | custom-call | tf_op jit(solution)/shard_map/pallas_call | solution.py:272
  76.1 1.3 %copy.13 = bf16[16,512]{1,0:T(8,128)(2,1)} copy(bf16[16,512]{1,0:T(8,128)(2,1)} %get-tuple-element.8) | data formatting | bytes 32768
  77.4 0.0 copy-start.1
  77.4 1.9 %copy.14 = bf16[512,512]{1,0:T(8,128)(2,1)} copy(bf16[512,512]{1,0:T(8,128)(2,1)} %get-tuple-element.9) | data formatting | bytes 1048576
  79.3 0.0 copy-done.1
  79.3 0.0 copy-start
  79.3 0.8 copy.15
  80.1 0.4 copy-done
  80.6 0.8 copy.16
Async XLA Ops:
  77.4 1.9 %copy-start.1 = (bf16[512,512]{1,0:T(8,128)(2,1)S(1)}, bf16[512,512]{1,0:T(8,128)(2,1)}, u32[]{:S(2)}) copy-start(bf16[512,512]{1,0:T(8,128)(2,1)} %get-tuple-element.10) | copy-start | bytes 1572868
  79.3 1.2 %copy-start = (bf16[512,512]{1,0:T(8,128)(2,1)S(1)}, bf16[512,512]{1,0:T(8,128)(2,1)}, u32[]{:S(2)}) copy-start(bf16[512,512]{1,0:T(8,128)(2,1)} %get-tuple-element.11) | copy-start | bytes 1572868

commit v3 on v2

--- a/solution.py
+++ b/solution.py
@@ -10,6 +10,7 @@
 ROWS = (((0,), (0,)), ((), ()))
 
 OFF = (0, 1, 3, 2)
+NEG = (0, 2, 1, 3)
 
 
 class Sems:
@@ -20,7 +21,7 @@
         return self.names.setdefault(name, len(self.names))
 
 
-N_SEMS = 200
+N_SEMS = 320
 
 
 def swiglu_back(gate, up_proj, hid_grad):
@@ -35,7 +36,7 @@
 def kernel(
     in_ref, og_ref, wg_ref, wu_ref, wd_ref,
     dx_ref, dwg_ref, dwu_ref, dwd_ref,
-    XG, WG, WU, WD, WGT, WUT, WDT, PP, RX, Z, ZR, HGU, DXF, DXS, SR, YF, ZS, ZHR, OUT, DW,
+    XG, WG, WU, WD, WGT, WUT, WDT, PP, RX, Z, ZR, HGU, DXF, DXS, SR, YF, ZS, ZHR,
     send_sem, recv_sem, local_sem,
 ):
     row = lax.axis_index("row")
@@ -88,15 +89,14 @@
         loads.append(c)
 
     barrier = pltpu.get_barrier_semaphore()
-    peers = [sib] + [ypeer(d, c) for d in (1, 2, 3) for c in (0, 1)] + [hpeer(d) for d in (1, 2, 3)]
-    peers += [xpeer(1), xpeer(3)] + [lpeer(d) for d in (1, 2, 3)]
+    peers = [sib] + [ypeer(d, c) for d in (1, 2, 3) for c in (0, 1)] + [hpeer(d) for d in (1, 3)]
+    peers += [xpeer(d) for d in (1, 2, 3)] + [lpeer(d) for d in (1, 2, 3)]
     for p in peers:
         pl.semaphore_signal(barrier, inc=1, device_id=p, device_id_type=pl.DeviceIdType.MESH)
     pl.semaphore_wait(barrier, len(peers))
     loads[0].wait()
     loads[1].wait()
 
-    NEG = (0, 2, 1, 3)
 
     def spread(k):
         src = XG.at[:, k, 0, 0]
@@ -106,11 +106,19 @@
         send("s%d" % k, src, XG.at[:, k, 1, 0], sib)
 
     spread(0)
-    for s in (1, 2, 3):
+    for s in (1, 2):
         send("h%d" % s, XG.at[:, 0, 0, 0], XG.at[:, NEG[s], 0, 0], hpeer(OFF[s]))
 
     def a_z(k):
-        recv("h%d" % NEG[k])
+        if k == 3:
+            recv("h30")
+            recv("h31")
+        else:
+            recv("h%d" % NEG[k])
+        if k == 2:
+            send("h30", XG.at[0, 2, 0, 0], XG.at[0, 3, 0, 0], hpeer(1))
+        if k == 1:
+            send("h31", XG.at[1, 1, 0, 0], XG.at[1, 3, 0, 0], hpeer(3))
         spread(k)
 
     def weights():
@@ -142,25 +150,15 @@
             for q in range(4):
                 PP[k, :, :, q, :, 128 * i:128 * (i + 1)] = (
                     part[:, 128 * q:128 * (q + 1)].reshape(4, 2, 16, 128))
-        send("far+%d" % k, PP.at[k, xf, 0], RX.at[k, 0], xpeer(1))
-        send("far-%d" % k, PP.at[k, xf, 1], RX.at[k, 1], xpeer(3))
-        send("dir+%d" % k, PP.at[k, xp, 1], RX.at[k, 4], xpeer(1))
-        send("dir-%d" % k, PP.at[k, xm, 0], RX.at[k, 3], xpeer(3))
-
-    def s2(k):
-        recv("far+%d" % k)
-        PP[k, xp, 0] = (PP[k, xp, 0].astype(F32) + RX[k, 0].astype(F32)).astype(BF16)
-        send("acc+%d" % k, PP.at[k, xp, 0], RX.at[k, 2], xpeer(1))
-        recv("far-%d" % k)
-        PP[k, xm, 1] = (PP[k, xm, 1].astype(F32) + RX[k, 1].astype(F32)).astype(BF16)
-        send("acc-%d" % k, PP.at[k, xm, 1], RX.at[k, 5], xpeer(3))
+        send("far%d" % k, PP.at[k, xf], RX.at[k, 0], xpeer(2))
+        send("dir+%d" % k, PP.at[k, xp], RX.at[k, 1], xpeer(1))
+        send("dir-%d" % k, PP.at[k, xm], RX.at[k, 2], xpeer(3))
 
     def s3(k):
-        for n in ("dir+", "dir-", "acc+", "acc-"):
+        for n in ("far", "dir+", "dir-"):
             recv(n + str(k))
-        for h in range(2):
-            Z[k, h] = (PP[k, x, h].astype(F32) + RX[k, 2 + 2 * h].astype(F32)
-                       + RX[k, 3 + 2 * h].astype(F32)).astype(BF16)
+        Z[k] = (PP[k, x].astype(F32) + RX[k, 0].astype(F32) + RX[k, 1].astype(F32)
+                + RX[k, 2].astype(F32)).astype(BF16)
         for m in (1, 2, 3):
             send("z%d%d" % (m, k), Z.at[k, :, (zl + m) % 4], ZR.at[k, m - 1], lpeer(m))
 
@@ -174,24 +172,17 @@
         HGU[k, x, :, zl, :, 0:128] = hidden
         HGU[k, x, :, zl, :, 128:256] = gate_grad
         HGU[k, x, :, zl, :, 256:384] = up_grad
+        mine = HGU.at[k, x, :, zl]
         for m in (1, 2, 3):
-            mine = HGU.at[k, x, :, zl]
             send("g%d%d" % (m, k), mine, mine, lpeer(m))
 
     def s5(k):
         for m in (1, 2, 3):
             recv("g%d%d" % (m, k))
         mine = HGU.at[k, x]
+        send("ag%d" % k, mine, mine, xpeer(2))
         send("ag+%d" % k, mine, mine, xpeer(1))
         send("ag-%d" % k, mine, mine, xpeer(3))
-
-    def s6(k):
-        recv("ag+%d" % k)
-        fwd = HGU.at[k, xm, 0]
-        send("af+%d" % k, fwd, fwd, xpeer(1))
-        recv("ag-%d" % k)
-        fwd = HGU.at[k, xp, 1]
-        send("af-%d" % k, fwd, fwd, xpeer(3))
 
     def cols(k, i):
         lead = (128,) if not isinstance(k, slice) else (512,)
@@ -199,8 +190,8 @@
             [HGU[k, :, :, q, :, 128 * i:128 * (i + 1)].reshape(lead + (128,)) for q in range(4)], axis=-1)
 
     def s7(k):
-        recv("af+%d" % k)
-        recv("af-%d" % k)
+        for n in ("ag", "ag+", "ag-"):
+            recv(n + str(k))
         dx = (jnp.dot(cols(k, 1), WGT[...], preferred_element_type=F32)
               + jnp.dot(cols(k, 2), WUT[...], preferred_element_type=F32))
         DXF[k] = dx[:16]
@@ -228,52 +219,61 @@
         for k in (1, 2, 3):
             recv("t%d" % k)
             total += ZHR[k - 1].astype(F32)
-        OUT[...] = total.astype(BF16)
-        c = pltpu.make_async_copy(OUT, dx_ref, local_sem.at[8])
-        c.start()
-        stores.append(c)
-
-    stores = []
+        dx_ref[...] = total.astype(BF16)
 
     def wgrad(i):
         al = slice(None)
         X = XG[0].reshape(512, 512)
         G = XG[1].reshape(512, 512)
         a, b, out = ((cols(al, 0), G, dwd_ref), (X, cols(al, 1), dwg_ref), (X, cols(al, 2), dwu_ref))[i]
-        DW[i] = lax.dot_general(a, b, ROWS, preferred_element_type=F32).astype(BF16)
-        c = pltpu.make_async_copy(DW.at[i], out, local_sem.at[5 + i])
-        c.start()
-        stores.append(c)
+        out[...] = lax.dot_general(a, b, ROWS, preferred_element_type=F32).astype(BF16)
 
     stages = dict(
-        s1=s1, s2=s2, s3=s3, s4=s4, s5=s5, s6=s6, s7=s7, s8=s8, s9=lambda _: s9(),
+        s1=s1, s3=s3, s4=s4, s5=s5, s7=s7, s8=s8, s9=lambda _: s9(),
         az=a_z, w=lambda i: (weights, weights2)[i](), wg=wgrad,
     )
     for name, k in SCHED:
         stages[name](k)
     for d in started.values():
         d.wait_send()
-    for c in stores:
+
+
+SCHED = (
+    ("w", 0), ("s1", 0), ("az", 1), ("az", 2), ("az", 3), ("w", 1), ("s1", 1), ("s3", 0), ("s1", 2),
+    ("s1", 3), ("s4", 0), ("s3", 1), ("s3", 2), ("s5", 0), ("s4", 1), ("s3", 3), ("s4", 2), ("s5", 1),
+    ("s4", 3), ("s5", 2), ("s7", 0), ("s5", 3), ("s7", 1), ("s8", 0), ("s7", 2), ("s8", 1), ("s7", 3),
+    ("wg", 0), ("s8", 2), ("s8", 3), ("wg", 1), ("wg", 2), ("s9", 0),
+)
+
+
+def copy_kernel(a, b, c, d, oa, ob, oc, od, sem):
+    copies = [pltpu.make_async_copy(s, t, sem.at[i]) for i, (s, t) in enumerate(((a, oa), (b, ob), (c, oc), (d, od)))]
+    for c in copies:
+        c.start()
+    for c in copies:
         c.wait()
 
 
-SCHED = (
-    ("w", 0), ("s1", 0), ("az", 1), ("az", 2), ("s2", 0), ("az", 3), ("w", 1),
-    ("s1", 1), ("s3", 0), ("s1", 2), ("s2", 1), ("s1", 3), ("s2", 2), ("s4", 0), ("s3", 1), ("s2", 3),
-    ("s3", 2), ("s5", 0), ("s4", 1), ("s3", 3), ("s4", 2), ("s6", 0), ("s5", 1), ("s4", 3), ("s5", 2),
-    ("s7", 0), ("s6", 1), ("s5", 3), ("s6", 2), ("s7", 1), ("s6", 3), ("s8", 0), ("s7", 2), ("s8", 1),
-    ("s7", 3), ("wg", 0), ("s8", 2), ("s8", 3), ("wg", 1), ("wg", 2), ("s9", 0),
-)
+def write_out(outs):
+    any_spec = pl.BlockSpec(memory_space=pl.ANY)
+    return tuple(pl.pallas_call(
+        copy_kernel,
+        out_shape=tuple(pltpu.HBM(o.shape, o.dtype) for o in outs),
+        in_specs=[any_spec] * 4,
+        out_specs=(any_spec,) * 4,
+        scratch_shapes=[pltpu.SemaphoreType.DMA((4,))],
+        name="write_out",
+    )(*[pltpu.with_memory_space_constraint(o, pltpu.VMEM) for o in outs]))
 
 
 def body(inputs, out_grad, gate_weight, up_weight, down_weight):
-    any_spec = pl.BlockSpec(memory_space=pl.ANY)
-    S = jax.ShapeDtypeStruct
-    return tuple(pl.pallas_call(
+    args = [pltpu.with_memory_space_constraint(a, pltpu.HBM)
+            for a in (inputs, out_grad, gate_weight, up_weight, down_weight)]
+    outs = pl.pallas_call(
         kernel,
-        out_shape=(S((16, 512), BF16), S((512, 512), BF16), S((512, 512), BF16), S((512, 512), BF16)),
-        in_specs=[pl.BlockSpec(memory_space=pltpu.HBM)] * 5,
-        out_specs=(any_spec,) * 4,
+        out_shape=(pltpu.VMEM((16, 512), BF16),) + (pltpu.VMEM((512, 512), BF16),) * 3,
+        in_specs=[pl.BlockSpec(memory_space=pl.ANY)] * 5,
+        out_specs=(pl.BlockSpec(memory_space=pltpu.VMEM),) * 4,
         scratch_shapes=[
             pltpu.VMEM((2, 4, 2, 4, 16, 512), BF16),
             pltpu.VMEM((512, 512), BF16),
@@ -283,7 +283,7 @@
             pltpu.VMEM((512, 512), BF16),
             pltpu.VMEM((512, 512), BF16),
             pltpu.VMEM((4, 4, 2, 4, 16, 384), BF16),
-            pltpu.VMEM((4, 6, 4, 16, 384), BF16),
+            pltpu.VMEM((4, 3, 2, 4, 16, 384), BF16),
             pltpu.VMEM((4, 2, 4, 16, 384), BF16),
             pltpu.VMEM((4, 3, 2, 16, 384), BF16),
             pltpu.VMEM((4, 4, 2, 4, 16, 384), BF16),
@@ -293,15 +293,14 @@
             pltpu.VMEM((16, 512), F32),
             pltpu.VMEM((3, 16, 512), BF16),
             pltpu.VMEM((3, 16, 512), BF16),
-            pltpu.VMEM((16, 512), BF16),
-            pltpu.VMEM((3, 512, 512), BF16),
             pltpu.SemaphoreType.DMA((N_SEMS,)),
             pltpu.SemaphoreType.DMA((N_SEMS,)),
-            pltpu.SemaphoreType.DMA((9,)),
+            pltpu.SemaphoreType.DMA((5,)),
         ],
         compiler_params=pltpu.CompilerParams(
-            collective_id=0, has_side_effects=True, vmem_limit_bytes=60 * 1024 * 1024),
-    )(inputs, out_grad, gate_weight, up_weight, down_weight))
+            collective_id=0, has_side_effects=True, vmem_limit_bytes=40 * 1024 * 1024),
+    )(*args)
+    return write_out(outs)
 
 
 def solution(mesh):

time: 81.6 us -> 77.1 us (0.945)
  local copies, waits for them, and re-layouts: 5.28 us -> 0 us
  Pallas kernels: 75.4 us -> 76.3 us
    unnamed x8 -> x0, local copies, waits for them, and re-layouts: 5.28 us -> none
    pallas_call x1 -> x2, Pallas kernels: 75.4 us -> 76.3 us  [the longest x1 75.1 us: body(): pl.pallas_call(kernel, out_shape=(pltpu.VMEM((16, 512), BF16),) + (pltpu....]
where the time goes in v3:
time: 77.1 us; the launch traced here: 76.9 us
  Pallas kernels  76.3 us (99%)
    pallas_call x1, Pallas kernels, body(): pl.pallas_call(kernel, out_shape=(pltpu.VMEM((16, 512), BF16),) + (pltpu....  75.1 us

profile of v3, /device:TPU:1, one launch (start us, length us, event | category | flops | bytes accessed | tf_op | source)
XLA Modules:
  0.0 76.9 jit_solution(11245494506763746898)
XLA Ops:
  0.6 75.1 %shard_map.84 = (bf16[16,512]{1,0:T(8,128)(2,1)S(1)}, bf16[512,512]{1,0:T(8,128)(2,1)S(1)}, bf16[512,512]{1,0:T(8,128)(2,1)S(1)}, bf16[512,512]{1,0:T(8,128)(2,1)S(1)}) custom-call(bf16[16,512]{1,0:T(8,128)(2,1)} %in_ref.1, bf16[16,512]{1,0:T(8,128)(2,1)} %og_ref.1, bf16[512,512]{1,0:T(8,128)(2,1)} %wg_ref.1, bf16[512,512]{1,0:T(8,128)(2,1)} %wu_ref.1, ...), custom_call_target="tpu_custom_call" | custom-call | tf_op jit(solution)/shard_map/pallas_call | solution.py:272
  75.8 1.2 %write_out.1 = (bf16[16,512]{1,0:T(8,128)(2,1)}, bf16[512,512]{1,0:T(8,128)(2,1)}, bf16[512,512]{1,0:T(8,128)(2,1)}, bf16[512,512]{1,0:T(8,128)(2,1)}) custom-call(bf16[16,512]{1,0:T(8,128)(2,1)S(1)} %get-tuple-element.8.a, bf16[512,512]{1,0:T(8,128)(2,1)S(1)} %get-tuple-element.9.b, bf16[512,512]{1,0:T(8,128)(2,1)S(1)} %get-tuple-element.10.c, ...), custom_call_target="tpu_custom_call" | custom-call | tf_op jit(solution)/shard_map/write_out/pallas_call | solution.py:259

commit v4 on v3

--- a/solution.py
+++ b/solution.py
@@ -79,6 +79,11 @@
     def recv(name):
         started[name].wait_recv()
 
+    barrier = pltpu.get_barrier_semaphore()
+    peers = [sib] + [ypeer(d, c) for d in (1, 2, 3) for c in (0, 1)] + [hpeer(d) for d in (1, 3)]
+    peers += [xpeer(d) for d in (1, 2, 3)] + [lpeer(d) for d in (1, 2, 3)]
+    for p in peers:
+        pl.semaphore_signal(barrier, inc=1, device_id=p, device_id_type=pl.DeviceIdType.MESH)
     loads = []
     for i, (src, dst) in enumerate((
         (in_ref, XG.at[0, 0, 0, 0]), (og_ref, XG.at[1, 0, 0, 0]),
@@ -88,11 +93,6 @@
         c.start()
         loads.append(c)
 
-    barrier = pltpu.get_barrier_semaphore()
-    peers = [sib] + [ypeer(d, c) for d in (1, 2, 3) for c in (0, 1)] + [hpeer(d) for d in (1, 3)]
-    peers += [xpeer(d) for d in (1, 2, 3)] + [lpeer(d) for d in (1, 2, 3)]
-    for p in peers:
-        pl.semaphore_signal(barrier, inc=1, device_id=p, device_id_type=pl.DeviceIdType.MESH)
     pl.semaphore_wait(barrier, len(peers))
     loads[0].wait()
     loads[1].wait()
@@ -239,10 +239,10 @@
 
 
 SCHED = (
-    ("w", 0), ("s1", 0), ("az", 1), ("az", 2), ("az", 3), ("w", 1), ("s1", 1), ("s3", 0), ("s1", 2),
-    ("s1", 3), ("s4", 0), ("s3", 1), ("s3", 2), ("s5", 0), ("s4", 1), ("s3", 3), ("s4", 2), ("s5", 1),
-    ("s4", 3), ("s5", 2), ("s7", 0), ("s5", 3), ("s7", 1), ("s8", 0), ("s7", 2), ("s8", 1), ("s7", 3),
-    ("wg", 0), ("s8", 2), ("s8", 3), ("wg", 1), ("wg", 2), ("s9", 0),
+    ("w", 0), ("s1", 0), ("az", 1), ("az", 2), ("az", 3), ("w", 1), ("s1", 1), ("s3", 0), ("s1", 3),
+    ("s1", 2), ("s4", 0), ("s3", 1), ("s3", 3), ("s5", 0), ("s4", 1), ("s3", 2), ("s4", 3), ("s5", 1),
+    ("s4", 2), ("s5", 3), ("s7", 0), ("s5", 2), ("s7", 1), ("s8", 0), ("s7", 3), ("s8", 1), ("s7", 2),
+    ("wg", 0), ("s8", 3), ("s8", 2), ("wg", 1), ("wg", 2), ("s9", 0),
 )
 
 

time: 77.1 us -> 76.6 us (level)
  no operation moved by 1% of the time
where the time goes in v4:
time: 76.6 us; the launch traced here: 76.4 us
  Pallas kernels  75.8 us (99%)
    pallas_call x1, Pallas kernels, body(): pl.pallas_call(kernel, out_shape=(pltpu.VMEM((16, 512), BF16),) + (pltpu....  74.6 us

profile of v4, /device:TPU:1, one launch (start us, length us, event | category | flops | bytes accessed | tf_op | source)
XLA Modules:
  0.0 76.4 jit_solution(1150405381702755976)
XLA Ops:
  0.6 74.6 %shard_map.84 = (bf16[16,512]{1,0:T(8,128)(2,1)S(1)}, bf16[512,512]{1,0:T(8,128)(2,1)S(1)}, bf16[512,512]{1,0:T(8,128)(2,1)S(1)}, bf16[512,512]{1,0:T(8,128)(2,1)S(1)}) custom-call(bf16[16,512]{1,0:T(8,128)(2,1)} %in_ref.1, bf16[16,512]{1,0:T(8,128)(2,1)} %og_ref.1, bf16[512,512]{1,0:T(8,128)(2,1)} %wg_ref.1, bf16[512,512]{1,0:T(8,128)(2,1)} %wu_ref.1, ...), custom_call_target="tpu_custom_call" | custom-call | tf_op jit(solution)/shard_map/pallas_call | solution.py:272
  75.3 1.2 %write_out.1 = (bf16[16,512]{1,0:T(8,128)(2,1)}, bf16[512,512]{1,0:T(8,128)(2,1)}, bf16[512,512]{1,0:T(8,128)(2,1)}, bf16[512,512]{1,0:T(8,128)(2,1)}) custom-call(bf16[16,512]{1,0:T(8,128)(2,1)S(1)} %get-tuple-element.8.a, bf16[512,512]{1,0:T(8,128)(2,1)S(1)} %get-tuple-element.9.b, bf16[512,512]{1,0:T(8,128)(2,1)S(1)} %get-tuple-element.10.c, ...), custom_call_target="tpu_custom_call" | custom-call | tf_op jit(solution)/shard_map/write_out/pallas_call | solution.py:259

commit v5 on v4

--- a/solution.py
+++ b/solution.py
@@ -133,13 +133,14 @@
     xp, xm = (x + 1) % 4, (x + 3) % 4
     xf = (x + 2) % 4
 
-    def s1(k):
-        for c in (0, 1):
-            for t in (1, 2, 3):
-                recv("y%d%d%d" % (k, c, t))
-        recv("s%d" % k)
-        xk = XG[0, k].reshape(128, 512)
-        gk = XG[1, k].reshape(128, 512)
+    def s1(g):
+        k, u = g
+        for t in (1, 2, 3):
+            recv("y%d%d%d" % (k, u, t))
+        if u:
+            recv("s%d" % k)
+        xk = XG[0, k, u].reshape(64, 512)
+        gk = XG[1, k, u].reshape(64, 512)
         parts = (
             jnp.dot(xk, WG[...], preferred_element_type=F32),
             jnp.dot(xk, WU[...], preferred_element_type=F32),
@@ -148,58 +149,65 @@
         for i, part in enumerate(parts):
             part = part.astype(BF16)
             for q in range(4):
-                PP[k, :, :, q, :, 128 * i:128 * (i + 1)] = (
-                    part[:, 128 * q:128 * (q + 1)].reshape(4, 2, 16, 128))
-        send("far%d" % k, PP.at[k, xf], RX.at[k, 0], xpeer(2))
-        send("dir+%d" % k, PP.at[k, xp], RX.at[k, 1], xpeer(1))
-        send("dir-%d" % k, PP.at[k, xm], RX.at[k, 2], xpeer(3))
-
-    def s3(k):
+                PP[k, u, :, q, :, 128 * i:128 * (i + 1)] = (
+                    part[:, 128 * q:128 * (q + 1)].reshape(4, 16, 128))
+        send("far%d%d" % g, PP.at[k, u, xf], RX.at[k, u, 0], xpeer(2))
+        send("dir+%d%d" % g, PP.at[k, u, xp], RX.at[k, u, 1], xpeer(1))
+        send("dir-%d%d" % g, PP.at[k, u, xm], RX.at[k, u, 2], xpeer(3))
+
+    def s3(g):
+        k, u = g
         for n in ("far", "dir+", "dir-"):
-            recv(n + str(k))
-        Z[k] = (PP[k, x].astype(F32) + RX[k, 0].astype(F32) + RX[k, 1].astype(F32)
-                + RX[k, 2].astype(F32)).astype(BF16)
+            recv(n + "%d%d" % g)
+        Z[k, u] = (PP[k, u, x].astype(F32) + RX[k, u, 0].astype(F32) + RX[k, u, 1].astype(F32)
+                   + RX[k, u, 2].astype(F32)).astype(BF16)
         for m in (1, 2, 3):
-            send("z%d%d" % (m, k), Z.at[k, :, (zl + m) % 4], ZR.at[k, m - 1], lpeer(m))
-
-    def s4(k):
+            send("z%d%d%d" % (m, k, u), Z.at[k, u, (zl + m) % 4], ZR.at[k, u, m - 1], lpeer(m))
+
+    def s4(g):
+        k, u = g
         for m in (1, 2, 3):
-            recv("z%d%d" % (m, k))
-        total = (Z[k, :, zl].astype(F32) + ZR[k, 0].astype(F32)
-                 + ZR[k, 1].astype(F32) + ZR[k, 2].astype(F32))
-        hidden, gate_grad, up_grad = swiglu_back(
-            total[:, :, :128], total[:, :, 128:256], total[:, :, 256:])
-        HGU[k, x, :, zl, :, 0:128] = hidden
-        HGU[k, x, :, zl, :, 128:256] = gate_grad
-        HGU[k, x, :, zl, :, 256:384] = up_grad
-        mine = HGU.at[k, x, :, zl]
+            recv("z%d%d%d" % (m, k, u))
+        total = (Z[k, u, zl].astype(F32) + ZR[k, u, 0].astype(F32)
+                 + ZR[k, u, 1].astype(F32) + ZR[k, u, 2].astype(F32))
+        hidden, gate_grad, up_grad = swiglu_back(total[:, :128], total[:, 128:256], total[:, 256:])
+        HGU[k, u, x, zl, :, 0:128] = hidden
+        HGU[k, u, x, zl, :, 128:256] = gate_grad
+        HGU[k, u, x, zl, :, 256:384] = up_grad
+        mine = HGU.at[k, u, x, zl]
         for m in (1, 2, 3):
-            send("g%d%d" % (m, k), mine, mine, lpeer(m))
-
-    def s5(k):
+            send("g%d%d%d" % (m, k, u), mine, mine, lpeer(m))
+
+    def s5(g):
+        k, u = g
         for m in (1, 2, 3):
-            recv("g%d%d" % (m, k))
-        mine = HGU.at[k, x]
-        send("ag%d" % k, mine, mine, xpeer(2))
-        send("ag+%d" % k, mine, mine, xpeer(1))
-        send("ag-%d" % k, mine, mine, xpeer(3))
-
-    def cols(k, i):
-        lead = (128,) if not isinstance(k, slice) else (512,)
+            recv("g%d%d%d" % (m, k, u))
+        mine = HGU.at[k, u, x]
+        send("ag%d%d" % g, mine, mine, xpeer(2))
+        send("ag+%d%d" % g, mine, mine, xpeer(1))
+        send("ag-%d%d" % g, mine, mine, xpeer(3))
+
+    def cols(i):
         return jnp.concatenate(
-            [HGU[k, :, :, q, :, 128 * i:128 * (i + 1)].reshape(lead + (128,)) for q in range(4)], axis=-1)
-
-    def s7(k):
+            [HGU[:, :, :, q, :, 128 * i:128 * (i + 1)].reshape(512, 128) for q in range(4)], axis=-1)
+
+    def s7(g):
+        k, u = g
         for n in ("ag", "ag+", "ag-"):
-            recv(n + str(k))
-        dx = (jnp.dot(cols(k, 1), WGT[...], preferred_element_type=F32)
-              + jnp.dot(cols(k, 2), WUT[...], preferred_element_type=F32))
-        DXF[k] = dx[:16]
-        DXS[k] = dx.astype(BF16).reshape(2, 4, 16, 512)
-        for c in (0, 1):
-            for s in (1, 2, 3):
-                send("f%d%d%d" % (k, c, s), DXS.at[k, c, s], SR.at[k, c, NEG[s]], ypeer(OFF[s], c))
-        send("f%d" % k, DXS.at[k, 1, 0], SR.at[k, 1, 0], sib)
+            recv(n + "%d%d" % g)
+        gate_grad, up_grad = (
+            jnp.concatenate(
+                [HGU[k, u, :, q, :, 128 * i:128 * (i + 1)].reshape(64, 128) for q in range(4)], axis=-1)
+            for i in (1, 2))
+        dx = (jnp.dot(gate_grad, WGT[...], preferred_element_type=F32)
+              + jnp.dot(up_grad, WUT[...], preferred_element_type=F32))
+        if u == 0:
+            DXF[k] = dx[:16]
+        DXS[k, u] = dx.astype(BF16).reshape(4, 16, 512)
+        for s in (1, 2, 3):
+            send("f%d%d%d" % (k, u, s), DXS.at[k, u, s], SR.at[k, u, NEG[s]], ypeer(OFF[s], u))
+        if u:
+            send("f%d" % k, DXS.at[k, 1, 0], SR.at[k, 1, 0], sib)
 
     def s8(k):
         recv("f%d" % k)
@@ -222,10 +230,9 @@
         dx_ref[...] = total.astype(BF16)
 
     def wgrad(i):
-        al = slice(None)
         X = XG[0].reshape(512, 512)
         G = XG[1].reshape(512, 512)
-        a, b, out = ((cols(al, 0), G, dwd_ref), (X, cols(al, 1), dwg_ref), (X, cols(al, 2), dwu_ref))[i]
+        a, b, out = ((cols(0), G, dwd_ref), (X, cols(1), dwg_ref), (X, cols(2), dwu_ref))[i]
         out[...] = lax.dot_general(a, b, ROWS, preferred_element_type=F32).astype(BF16)
 
     stages = dict(
@@ -239,10 +246,14 @@
 
 
 SCHED = (
-    ("w", 0), ("s1", 0), ("az", 1), ("az", 2), ("az", 3), ("w", 1), ("s1", 1), ("s3", 0), ("s1", 3),
-    ("s1", 2), ("s4", 0), ("s3", 1), ("s3", 3), ("s5", 0), ("s4", 1), ("s3", 2), ("s4", 3), ("s5", 1),
-    ("s4", 2), ("s5", 3), ("s7", 0), ("s5", 2), ("s7", 1), ("s8", 0), ("s7", 3), ("s8", 1), ("s7", 2),
-    ("wg", 0), ("s8", 3), ("s8", 2), ("wg", 1), ("wg", 2), ("s9", 0),
+    ("w", 0), ("w", 1), ("s1", (0, 0)), ("s1", (0, 1)), ("az", 2), ("az", 1), ("s1", (2, 0)), ("az", 3),
+    ("s1", (2, 1)), ("s1", (1, 0)), ("s3", (2, 0)), ("s3", (0, 1)), ("s1", (3, 0)), ("s3", (2, 1)),
+    ("s1", (3, 1)), ("s3", (1, 0)), ("s4", (0, 1)), ("s4", (2, 0)), ("s1", (1, 1)), ("s3", (3, 0)),
+    ("s4", (2, 1)), ("s3", (0, 0)), ("s3", (3, 1)), ("s5", (0, 1)), ("s5", (2, 0)), ("s3", (1, 1)),
+    ("s4", (3, 0)), ("s5", (2, 1)), ("s4", (0, 0)), ("s4", (3, 1)), ("s4", (1, 0)), ("s4", (1, 1)),
+    ("s5", (3, 0)), ("s5", (3, 1)), ("s5", (1, 0)), ("s7", (2, 0)), ("s7", (0, 1)), ("s5", (1, 1)),
+    ("s7", (3, 0)), ("s7", (2, 1)), ("s5", (0, 0)), ("s7", (3, 1)), ("s7", (1, 0)), ("s8", 3), ("s7", (1, 1)),
+    ("s7", (0, 0)), ("s8", 2), ("s8", 1), ("wg", 2), ("wg", 0), ("wg", 1), ("s8", 0), ("s9", 0),
 )
 
 
@@ -282,11 +293,11 @@
             pltpu.VMEM((512, 512), BF16),
             pltpu.VMEM((512, 512), BF16),
             pltpu.VMEM((512, 512), BF16),
-            pltpu.VMEM((4, 4, 2, 4, 16, 384), BF16),
-            pltpu.VMEM((4, 3, 2, 4, 16, 384), BF16),
+            pltpu.VMEM((4, 2, 4, 4, 16, 384), BF16),
+            pltpu.VMEM((4, 2, 3, 4, 16, 384), BF16),
             pltpu.VMEM((4, 2, 4, 16, 384), BF16),
-            pltpu.VMEM((4, 3, 2, 16, 384), BF16),
-            pltpu.VMEM((4, 4, 2, 4, 16, 384), BF16),
+            pltpu.VMEM((4, 2, 3, 16, 384), BF16),
+            pltpu.VMEM((4, 2, 4, 4, 16, 384), BF16),
             pltpu.VMEM((4, 16, 512), F32),
             pltpu.VMEM((4, 2, 4, 16, 512), BF16),
             pltpu.VMEM((4, 2, 4, 16, 512), BF16),

time: 76.6 us -> 73.9 us (0.965)
  Pallas kernels: 75.8 us -> 73.1 us
    pallas_call x1, Pallas kernels: 74.6 us -> 71.9 us  [body(): pl.pallas_call(kernel, out_shape=(pltpu.VMEM((16, 512), BF16),) + (pltpu....]
where the time goes in v5:
time: 73.9 us; the launch traced here: 73.8 us
  Pallas kernels  73.1 us (99%)
    pallas_call x1, Pallas kernels, body(): pl.pallas_call(kernel, out_shape=(pltpu.VMEM((16, 512), BF16),) + (pltpu....  71.9 us

profile of v5, /device:TPU:1, one launch (start us, length us, event | category | flops | bytes accessed | tf_op | source)
XLA Modules:
  0.0 73.8 jit_solution(14576479611795131196)
XLA Ops:
  0.6 71.9 %shard_map.84 = (bf16[16,512]{1,0:T(8,128)(2,1)S(1)}, bf16[512,512]{1,0:T(8,128)(2,1)S(1)}, bf16[512,512]{1,0:T(8,128)(2,1)S(1)}, bf16[512,512]{1,0:T(8,128)(2,1)S(1)}) custom-call(bf16[16,512]{1,0:T(8,128)(2,1)} %in_ref.1, bf16[16,512]{1,0:T(8,128)(2,1)} %og_ref.1, bf16[512,512]{1,0:T(8,128)(2,1)} %wg_ref.1, bf16[512,512]{1,0:T(8,128)(2,1)} %wu_ref.1, ...), custom_call_target="tpu_custom_call" | custom-call | tf_op jit(solution)/shard_map/pallas_call | solution.py:283
  72.6 1.2 %write_out.1 = (bf16[16,512]{1,0:T(8,128)(2,1)}, bf16[512,512]{1,0:T(8,128)(2,1)}, bf16[512,512]{1,0:T(8,128)(2,1)}, bf16[512,512]{1,0:T(8,128)(2,1)}) custom-call(bf16[16,512]{1,0:T(8,128)(2,1)S(1)} %get-tuple-element.8.a, bf16[512,512]{1,0:T(8,128)(2,1)S(1)} %get-tuple-element.9.b, bf16[512,512]{1,0:T(8,128)(2,1)S(1)} %get-tuple-element.10.c, ...), custom_call_target="tpu_custom_call" | custom-call | tf_op jit(solution)/shard_map/write_out/pallas_call | solution.py:270

commit v6 on v5

--- a/solution.py
+++ b/solution.py
@@ -100,9 +100,8 @@
 
     def spread(k):
         src = XG.at[:, k, 0, 0]
-        for c in (0, 1):
-            for s in (1, 2, 3):
-                send("y%d%d%d" % (k, c, s), src, XG.at[:, k, c, NEG[s]], ypeer(OFF[s], c))
+        for s in (1, 2, 3):
+            send("y%d0%d" % (k, s), src, XG.at[:, k, 0, NEG[s]], ypeer(OFF[s]))
         send("s%d" % k, src, XG.at[:, k, 1, 0], sib)
 
     spread(0)
@@ -135,10 +134,13 @@
 
     def s1(g):
         k, u = g
-        for t in (1, 2, 3):
-            recv("y%d%d%d" % (k, u, t))
         if u:
+            recv("rl%d" % k)
             recv("s%d" % k)
+        else:
+            for t in (1, 2, 3):
+                recv("y%d0%d" % (k, t))
+            send("rl%d" % k, XG.at[:, k, 0, pl.ds(1, 3)], XG.at[:, k, 1, pl.ds(1, 3)], sib)
         xk = XG[0, k, u].reshape(64, 512)
         gk = XG[1, k, u].reshape(64, 512)
         parts = (

time: 73.9 us -> 73.8 us (level)
  no operation moved by 1% of the time
where the time goes in v6:
time: 73.8 us; the launch traced here: 73.7 us
  Pallas kernels  73 us (99%)
    pallas_call x1, Pallas kernels, body(): pl.pallas_call(kernel, out_shape=(pltpu.VMEM((16, 512), BF16),) + (pltpu....  71.8 us

profile of v6, /device:TPU:1, one launch (start us, length us, event | category | flops | bytes accessed | tf_op | source)
XLA Modules:
  0.0 73.7 jit_solution(687845639537226423)
XLA Ops:
  0.6 71.8 %shard_map.84 = (bf16[16,512]{1,0:T(8,128)(2,1)S(1)}, bf16[512,512]{1,0:T(8,128)(2,1)S(1)}, bf16[512,512]{1,0:T(8,128)(2,1)S(1)}, bf16[512,512]{1,0:T(8,128)(2,1)S(1)}) custom-call(bf16[16,512]{1,0:T(8,128)(2,1)} %in_ref.1, bf16[16,512]{1,0:T(8,128)(2,1)} %og_ref.1, bf16[512,512]{1,0:T(8,128)(2,1)} %wg_ref.1, bf16[512,512]{1,0:T(8,128)(2,1)} %wu_ref.1, ...), custom_call_target="tpu_custom_call" | custom-call | tf_op jit(solution)/shard_map/pallas_call | solution.py:285
  72.5 1.2 %write_out.1 = (bf16[16,512]{1,0:T(8,128)(2,1)}, bf16[512,512]{1,0:T(8,128)(2,1)}, bf16[512,512]{1,0:T(8,128)(2,1)}, bf16[512,512]{1,0:T(8,128)(2,1)}) custom-call(bf16[16,512]{1,0:T(8,128)(2,1)S(1)} %get-tuple-element.8.a, bf16[512,512]{1,0:T(8,128)(2,1)S(1)} %get-tuple-element.9.b, bf16[512,512]{1,0:T(8,128)(2,1)S(1)} %get-tuple-element.10.c, ...), custom_call_target="tpu_custom_call" | custom-call | tf_op jit(solution)/shard_map/write_out/pallas_call | solution.py:272
